TPU v7x, 32 devices: a whole 2x2x4 slice. The times are simulated.
32 devices in a mesh: depth: 4 (over y, x), gx: 2 (over core), gy: 4 (over z).
Axes of the slice: x: 2, y: 2, z: 4, core: 2. Of those that a mesh axis runs over, the one named last changes fastest.
Arguments:
- density: float32 [16, 64, 1024], P('depth', 'gx', 'gy'), may hold values from 0.1 to 1
- table_index: int32 [16, 64, 1024], P('depth', 'gx', 'gy'), may hold values from 0 to 255
- opacity_table: float32 [256], replicated, may hold values from 0.02 to 0.3
- color_table: float32 [3, 256], replicated, may hold values from 0.5 to 3
- light_direction: float32 [4, 3], replicated, may hold values from -4 to 4
- shear_offsets: int32 [4, 16, 2], replicated, may hold values from -16 to 16, as said below
Outputs:
- image: float32 [4, 4, 64, 1024], P('depth', None, 'gx', 'gy')
Inputs may be any that keep to these rules, and one draw needn't show every extreme that they name: `shear_offsets`: every offset lies within -16 to 16; both ends occur in every draw.
All inputs are finite; a program needn't handle non-finite values.
Results may differ from a plain program's by a relative error of at most 0.000051.
Values sent between devices are 32-bit elements; how exact they have to be, the bound alone decides.
A program may use at most 64 MiB of HBM per device.

v0:
```python
import functools

import jax
import jax.numpy as jnp
from jax import lax
from jax.experimental import pallas as pl
from jax.experimental.pallas import tpu as pltpu
from jax.sharding import PartitionSpec as P

MAXS = 16
LANES = 128
SUB = 8
GROUP = 32

ambient = 0.3
diffuse = 0.7

STEPS = (-1, 0, 1)
DIRS = [(z, x, y) for z in STEPS for x in STEPS for y in STEPS if (z, x, y) != (0, 0, 0)]


def flipped(value, mask):
    bit = 1
    while bit <= mask:
        if mask & bit:
            value = value + bit - 2 * bit * ((value // bit) % 2)
        bit *= 2
    return value


def kernel(
    sizes, dens_in, index_in, opacity_in, color_in, light_in, shear_in, out,
    opacity, color, light, shear, in_sem, wide_d, wide_i, edges, got_edges, got_depth, shaded, parts, others, image,
    send_sem, recv_sem, send2, recv2, part_send, part_recv,
):
    nd, nx, ny = sizes
    slices, rows, cols = dens_in.shape
    tiles = cols // LANES
    wide = cols + LANES
    halo = -(-(MAXS + 1) // SUB) * SUB
    low, high = halo, halo + rows
    me = (lax.axis_index("depth"), lax.axis_index("gx"), lax.axis_index("gy"))
    d = me[0]

    def there(step):
        ok = None
        for pos, s, n in zip(me, step, sizes):
            if s:
                one = (pos + s < n) if s > 0 else (pos + s >= 0)
                ok = one if ok is None else jnp.logical_and(ok, one)
        return ok

    def dev(step):
        return tuple(pos + s for pos, s in zip(me, step))

    masks = list(range(nd - 1, 0, -1))
    barrier = pltpu.get_barrier_semaphore()
    count = jnp.int32(0)
    for step in DIRS:
        ok = there(step)

        @pl.when(ok)
        def _():
            pl.semaphore_signal(barrier, inc=1, device_id=dev(step), device_id_type=pl.DeviceIdType.MESH)

        count = count + jnp.where(ok, 1, 0)
    for mask in masks:
        gap = flipped(d, mask) - d
        far = jnp.logical_or(gap > 1, gap < -1)

        @pl.when(far)
        def _():
            pl.semaphore_signal(
                barrier, inc=1, device_id=(flipped(d, mask), me[1], me[2]),
                device_id_type=pl.DeviceIdType.MESH,
            )

        count = count + jnp.where(far, 1, 0)

    dens = wide_d.at[pl.ds(1, slices), pl.ds(low, rows), pl.ds(0, cols)]
    index = wide_i.at[:, pl.ds(low, rows), pl.ds(0, cols)]
    loads = [
        pltpu.make_async_copy(src, dst, in_sem.at[k])
        for k, (src, dst) in enumerate((
            (dens_in, dens), (index_in, index), (opacity_in, opacity), (color_in, color),
            (light_in, light), (shear_in, shear),
        ))
    ]
    for load in loads:
        load.start()
    loads[0].wait()
    loads[1].wait()
    lane = lax.broadcasted_iota(jnp.int32, (SUB, LANES), 1)
    group = lane // GROUP
    for side in range(2):
        tile = tiles - 1 if side == 0 else 0
        for number, (ref, buf) in enumerate(((wide_d, 0), (wide_i, 1))):
            for z in range(slices):
                packed = None
                for r in range(rows // SUB):
                    v = ref[z + 1 - buf, low + r * SUB:low + (r + 1) * SUB, tile * LANES:(tile + 1) * LANES]
                    shift = (GROUP * r + (GROUP if side == 0 else 0)) % LANES
                    v = pltpu.roll(v, shift, 1) if shift else v
                    packed = v if packed is None else jnp.where(group == r, v, packed)
                edges[buf][side, z] = packed

    def src_rows(x, reach):
        return pl.ds(high - reach, reach) if x > 0 else (pl.ds(low, reach) if x < 0 else pl.ds(low, rows))

    def dst_rows(x, reach):
        return pl.ds(low - reach, reach) if x > 0 else (pl.ds(high, reach) if x < 0 else pl.ds(low, rows))

    def copies(number, step, only_dst=False):
        z, x, y = step
        side = 0 if y > 0 else 1
        if z == 0 and y == 0:
            pairs = [
                (wide_d.at[pl.ds(1, slices), src_rows(x, halo), pl.ds(0, cols)],
                 wide_d.at[pl.ds(1, slices), dst_rows(x, halo), pl.ds(0, cols)]),
                (wide_i.at[:, src_rows(x, MAXS), pl.ds(0, cols)], wide_i.at[:, dst_rows(x, MAXS), pl.ds(0, cols)]),
            ]
        elif z == 0:
            pairs = [
                (edges[0].at[side], got_edges[0].at[x + 1, side]),
                (edges[1].at[side], got_edges[1].at[x + 1, side]),
            ]
        else:
            edge = slices - 1 if z > 0 else 0
            slot = 0 if z > 0 else 1
            if y == 0:
                pairs = [(
                    wide_d.at[edge + 1, src_rows(x, MAXS), pl.ds(0, cols)],
                    wide_d.at[0 if z > 0 else slices + 1, dst_rows(x, MAXS), pl.ds(0, cols)],
                )]
            else:
                pairs = [(edges[0].at[side, edge], got_depth.at[slot, x + 1, side])]
        if only_dst:
            return [dst for _src, dst in pairs]
        made = []
        for (src, dst), (ss, rs) in zip(pairs, ((send_sem, recv_sem), (send2, recv2))):
            made.append(pltpu.make_async_remote_copy(
                src_ref=src, dst_ref=dst, send_sem=ss.at[number], recv_sem=rs.at[number],
                device_id=dev(step), device_id_type=pl.DeviceIdType.MESH,
            ))
        return made

    pl.semaphore_wait(barrier, count)
    order = sorted(range(len(DIRS)), key=lambda k: -sum(abs(s) for s in DIRS[k]))
    for number in order:
        step = DIRS[number]

        @pl.when(there(step))
        def _():
            for copy in copies(number, step):
                copy.start()

    for number in order:
        step = DIRS[number]
        back = tuple(-s for s in step)

        @pl.when(jnp.logical_not(there(back)))
        def _():
            for dst in copies(number, step, only_dst=True):
                dst[...] = jnp.zeros(dst.shape, dst.dtype)

    for load in loads[2:]:
        load.wait()

    entries = opacity.shape[0] // LANES
    tables = []
    for name in range(4):
        halves = []
        for e in range(entries):
            if name == 0:
                row = opacity[e * LANES:(e + 1) * LANES].reshape(1, LANES)
            else:
                row = color[name - 1:name, e * LANES:(e + 1) * LANES]
            halves.append(jnp.broadcast_to(row, (SUB, LANES)))
        tables.append(halves)

    def look(name, low_bits, part):
        value = None
        for e in range(entries):
            g = jnp.take_along_axis(tables[name][e], low_bits, axis=1, mode="promise_in_bounds")
            value = g if value is None else jnp.where(part >= e, g, value)
        return value

    offset = halo - MAXS

    def look_up(z, t, j):
        at = offset + t * SUB
        r0 = t * SUB
        cut = slice(j * LANES, (j + 1) * LANES)
        i = wide_i[z, at:at + SUB, cut]
        low_bits = jnp.bitwise_and(i, LANES - 1)
        part = jnp.right_shift(i, 7)
        alpha = 1.0 - jnp.exp(-look(0, low_bits, part) * wide_d[z + 1, at:at + SUB, cut])
        shaded[0, z, j, r0:r0 + SUB, :] = alpha
        for ch in range(3):
            shaded[1 + ch, z, j, r0:r0 + SUB, :] = alpha * look(1 + ch, low_bits, part)

    def slopes(z):
        for t in range(wide_tiles):
            at = offset + t * SUB
            r0 = t * SUB
            c = wide_d[z + 1, at:at + SUB, :]
            sd = wide_d[z + 2, at:at + SUB, :] - wide_d[z, at:at + SUB, :]
            sx = wide_d[z + 1, at + 1:at + 1 + SUB, :] - wide_d[z + 1, at - 1:at - 1 + SUB, :]
            sy = pltpu.roll(c, wide - 1, 1) - pltpu.roll(c, 1, 1)
            inv = lax.rsqrt(0.25 * (sd * sd + sx * sx + sy * sy) + 1.0) * (0.5 * diffuse)
            for j in range(wide // LANES):
                for k, slope in enumerate((sd, sx, sy)):
                    shaded[4 + k, z, j, r0:r0 + SUB, :] = (slope * inv)[:, j * LANES:(j + 1) * LANES]

    wide_tiles = (rows + 2 * MAXS) // SUB
    own = [
        (t, j) for t in range(MAXS // SUB, (MAXS + rows) // SUB) for j in range(tiles)
    ]
    rest = [
        (t, j) for t in range(wide_tiles) for j in range(tiles + 1) if (t, j) not in own
    ]

    def over_slices(first, last, body):
        def step(z, carry):
            body(z)
            return carry

        lax.fori_loop(first, last, step, 0)

    def look_all(places):
        def body(z):
            for t, j in places:
                look_up(z, t, j)

        over_slices(0, slices, body)

    def arrive(depth):
        for number in reversed(order):
            step = DIRS[number]
            if (step[0] != 0) != depth:
                continue

            @pl.when(there(tuple(-s for s in step)))
            def _():
                for copy in copies(number, step):
                    copy.wait_recv()

    def unpack(depth):
        for x in STEPS:
            first, last = (rows - halo, rows) if x > 0 else ((0, halo) if x < 0 else (0, rows))
            base = 0 if x > 0 else (high if x < 0 else low)
            if depth:
                jobs = [
                    (got_depth.at[slot, x + 1], wide_d.at[slot * (slices + 1)]) for slot in range(2)
                ]
                jobs = [(got.at[0], got.at[1], target) for got, target in jobs]
            else:
                jobs = [
                    (got.at[x + 1, 0, z], got.at[x + 1, 1, z], target.at[z + skip])
                    for got, target, skip in ((got_edges[0], wide_d, 1), (got_edges[1], wide_i, 0))
                    for z in range(slices)
                ]
            for from_left, from_right, target in jobs:
                left, right = from_left[...], from_right[...]
                for r in range(first // SUB, last // SUB):
                    a = (LANES - GROUP * r) % LANES
                    b = (LANES - GROUP - GROUP * r) % LANES
                    rr = pltpu.roll(right, a, 1) if a else right
                    ll = pltpu.roll(left, b, 1) if b else left
                    at = base + r * SUB - first
                    target[at:at + SUB, cols:wide] = jnp.where(lane < LANES // 2, rr, ll)

    look_all(own)
    arrive(False)
    unpack(False)
    look_all(rest)
    over_slices(1, slices - 1, slopes)
    arrive(True)
    unpack(True)
    slopes(0)
    if slices > 1:
        slopes(slices - 1)

    def partial(mask, first, last):
        view = flipped(d, mask)
        l0, l1, l2 = (light[view, k] for k in range(3))
        moves = []
        for z in range(slices):
            px = shear[view, 0, d * slices + z]
            py = shear[view, 1, d * slices + z]
            moves.append((
                MAXS - px, jnp.where(py < 0, py + LANES, py), lane < py, lane >= py + LANES,
            ))

        def rows_of(t, carry):
            acc = [[jnp.zeros((SUB, LANES), jnp.float32) for _ in range(tiles)] for _ in range(4)]
            for z in range(slices):
                start, turn, from_low, from_high = moves[z]
                at = pl.ds(start + t * SUB, SUB)
                bright = [
                    ambient + jnp.abs(
                        l0 * shaded[4, z, j, at, :] + l1 * shaded[5, z, j, at, :]
                        + l2 * shaded[6, z, j, at, :]
                    )
                    for j in range(tiles + 1)
                ]
                through = [1.0 - a for a in acc[0]]
                for ch in range(4):
                    turned = []
                    for j in range(tiles + 1):
                        v = shaded[ch, z, j, at, :]
                        turned.append(pltpu.roll(v * bright[j] if ch else v, turn, 1))
                    for j in range(tiles):
                        moved = jnp.where(
                            from_low, turned[j - 1],
                            jnp.where(from_high, turned[j + 1], turned[j]),
                        )
                        acc[ch][j] = acc[ch][j] + through[j] * moved
            r = pl.multiple_of(t * SUB, SUB)
            for ch in range(4):
                for j in range(tiles):
                    parts[mask, ch, pl.ds(r, SUB), j * LANES:(j + 1) * LANES] = acc[ch][j]
            return carry

        lax.fori_loop(first, last, rows_of, 0)

    sent = []
    halves = 4
    part = rows // halves

    def cut(h):
        return pl.ds(h * part, part)

    for h in range(halves):
        for mask in masks:
            partial(mask, h * part // SUB, (h + 1) * part // SUB)
            copy = pltpu.make_async_remote_copy(
                src_ref=parts.at[mask, :, cut(h), :], dst_ref=others.at[mask, :, cut(h), :],
                send_sem=part_send.at[mask, h], recv_sem=part_recv.at[mask, h],
                device_id=(flipped(d, mask), me[1], me[2]), device_id_type=pl.DeviceIdType.MESH,
            )
            copy.start()
            sent.append(copy)
    partial(0, 0, rows // SUB)
    others[0] = parts[0]
    for number in order:
        step = DIRS[number]

        @pl.when(there(step))
        def _():
            for copy in copies(number, step):
                copy.wait_send()

    def finish(t, carry):
        r = pl.multiple_of(t * SUB, SUB)
        acc = None
        for j in range(nd):
            slot = sum(
                bit * ((d // bit + j // bit) % 2) for bit in (1 << k for k in range((nd - 1).bit_length()))
            ) if nd > 1 else 0
            new = [others[slot, ch, pl.ds(r, SUB), :] for ch in range(4)]
            if acc is None:
                acc = new
            else:
                through = 1.0 - acc[0]
                acc = [a + through * n for a, n in zip(acc, new)]
        for ch in range(4):
            image[0, ch, pl.ds(r, SUB), :] = acc[ch]
        return carry

    puts = []
    for h in range(halves):
        for copy in sent[h * len(masks):(h + 1) * len(masks)]:
            copy.wait_recv()
        lax.fori_loop(h * part // SUB, (h + 1) * part // SUB, finish, 0)
        put = pltpu.make_async_copy(
            image.at[:, :, cut(h), :], out.at[:, :, cut(h), :], in_sem.at[h]
        )
        put.start()
        puts.append(put)

    for copy in sent:
        copy.wait_send()
    for put in puts:
        put.wait()

def local(sizes, density, table_index, opacity_table, color_table, light_direction, shear_offsets):
    slices, rows, cols = density.shape
    views = light_direction.shape[0]
    nd = sizes[0]
    assert views == nd and rows // SUB * GROUP == LANES
    wide = cols + LANES
    halo = -(-(MAXS + 1) // SUB) * SUB
    f32, i32 = jnp.float32, jnp.int32
    dma = pltpu.SemaphoreType.DMA
    turned = jnp.transpose(shear_offsets, (0, 2, 1))
    return pl.pallas_call(
        functools.partial(kernel, sizes),
        out_shape=jax.ShapeDtypeStruct((1, 4, rows, cols), f32),
        in_specs=[pl.BlockSpec(memory_space=pl.ANY)] * 6,
        out_specs=pl.BlockSpec(memory_space=pl.ANY),
        scratch_shapes=[
            pltpu.VMEM(opacity_table.shape, f32),
            pltpu.VMEM(color_table.shape, f32),
            pltpu.SMEM(light_direction.shape, f32),
            pltpu.SMEM(turned.shape, i32),
            dma((6,)),
            pltpu.VMEM((slices + 2, rows + 2 * halo, wide), f32),
            pltpu.VMEM((slices, rows + 2 * halo, wide), i32),
            [pltpu.VMEM((2, slices, SUB, LANES), f32), pltpu.VMEM((2, slices, SUB, LANES), i32)],
            [pltpu.VMEM((3, 2, slices, SUB, LANES), f32), pltpu.VMEM((3, 2, slices, SUB, LANES), i32)],
            pltpu.VMEM((2, 3, 2, SUB, LANES), f32),
            pltpu.VMEM((7, slices, wide // LANES, rows + 2 * MAXS, LANES), f32),
            pltpu.VMEM((nd, 4, rows, cols), f32),
            pltpu.VMEM((nd, 4, rows, cols), f32),
            pltpu.VMEM((1, 4, rows, cols), f32),
            dma((len(DIRS),)), dma((len(DIRS),)), dma((len(DIRS),)), dma((len(DIRS),)),
            dma((nd, 4)), dma((nd, 4)),
        ],
        compiler_params=pltpu.CompilerParams(collective_id=0, has_side_effects=True),
    )(density, table_index, opacity_table, color_table, light_direction, turned)


def solution(mesh):
    sizes = tuple(mesh.shape[name] for name in ("depth", "gx", "gy"))
    return jax.shard_map(
        functools.partial(local, sizes),
        mesh=mesh,
        in_specs=(P("depth", "gx", "gy"), P("depth", "gx", "gy"), P(), P(), P(), P()),
        out_specs=P("depth", None, "gx", "gy"),
        check_vma=False,
    )
```

profile of v0, /device:TPU:0, one launch (start us, length us, event | category | flops | bytes accessed | tf_op | source)
XLA Modules:
  0.0 21.4 jit_solution(7310765282330346634)
XLA Ops:
  0.0 19.8 %shard_map.64 = f32[1,4,32,256]{3,2,1,0:T(8,128)} custom-call(f32[4,32,256]{2,1,0:T(8,128)} %dens_in.1, s32[4,32,256]{2,1,0:T(8,128)} %index_in.1, f32[256]{0:T(256)} %opacity_in.1, f32[3,256]{1,0:T(4,128)} %color_in.1, f32[4,3]{1,0:T(4,128)} %light_in.1, s32[4,2,16]{2,1,0:T(2,128)} %bitcast.1), custom_call_target="tpu_custom_call" | custom-call | tf_op jit(solution)/shard_map/pallas_call | solution.py:397
  19.8 1.6 %copy.8 = f32[1,4,32,256]{3,2,1,0:T(8,128)} copy(f32[1,4,32,256]{3,2,1,0:T(8,128)} %shard_map.64) | data formatting | bytes 262144
where the time goes:
time: 21.5 us; the launch traced here: 21.4 us
  Pallas kernels  19.8 us (92%)
  local copies, waits for them, and re-layouts  1.57 us (7%)
    pallas_call x1, Pallas kernels, local(): pl.pallas_call(functools.partial(kernel, sizes), out_shape=jax.ShapeDtype...  19.8 us
    unnamed x1, local copies, waits for them, and re-layouts  1.57 us

commit v1 on v0

--- a/solution.py
+++ b/solution.py
@@ -29,8 +29,8 @@
 
 
 def kernel(
-    sizes, dens_in, index_in, opacity_in, color_in, light_in, shear_in, out,
-    opacity, color, light, shear, in_sem, wide_d, wide_i, edges, got_edges, got_depth, shaded, parts, others, image,
+    sizes, dens_in, index_in, opacity_in, color_in, light_in, shear_in, others,
+    opacity, color, light, shear, in_sem, wide_d, wide_i, edges, got_edges, got_depth, shaded, parts,
     send_sem, recv_sem, send2, recv2, part_send, part_recv,
 ):
     nd, nx, ny = sizes
@@ -335,14 +335,15 @@
         for mask in masks:
             partial(mask, h * part // SUB, (h + 1) * part // SUB)
             copy = pltpu.make_async_remote_copy(
-                src_ref=parts.at[mask, :, cut(h), :], dst_ref=others.at[mask, :, cut(h), :],
+                src_ref=parts.at[mask, :, cut(h), :], dst_ref=others.at[d, :, cut(h), :],
                 send_sem=part_send.at[mask, h], recv_sem=part_recv.at[mask, h],
                 device_id=(flipped(d, mask), me[1], me[2]), device_id_type=pl.DeviceIdType.MESH,
             )
             copy.start()
             sent.append(copy)
     partial(0, 0, rows // SUB)
-    others[0] = parts[0]
+    keep = pltpu.make_async_copy(parts.at[0], others.at[d], in_sem.at[0])
+    keep.start()
     for number in order:
         step = DIRS[number]
 
@@ -351,38 +352,12 @@
             for copy in copies(number, step):
                 copy.wait_send()
 
-    def finish(t, carry):
-        r = pl.multiple_of(t * SUB, SUB)
-        acc = None
-        for j in range(nd):
-            slot = sum(
-                bit * ((d // bit + j // bit) % 2) for bit in (1 << k for k in range((nd - 1).bit_length()))
-            ) if nd > 1 else 0
-            new = [others[slot, ch, pl.ds(r, SUB), :] for ch in range(4)]
-            if acc is None:
-                acc = new
-            else:
-                through = 1.0 - acc[0]
-                acc = [a + through * n for a, n in zip(acc, new)]
-        for ch in range(4):
-            image[0, ch, pl.ds(r, SUB), :] = acc[ch]
-        return carry
-
-    puts = []
-    for h in range(halves):
-        for copy in sent[h * len(masks):(h + 1) * len(masks)]:
-            copy.wait_recv()
-        lax.fori_loop(h * part // SUB, (h + 1) * part // SUB, finish, 0)
-        put = pltpu.make_async_copy(
-            image.at[:, :, cut(h), :], out.at[:, :, cut(h), :], in_sem.at[h]
-        )
-        put.start()
-        puts.append(put)
-
+    for copy in sent:
+        copy.wait_recv()
     for copy in sent:
         copy.wait_send()
-    for put in puts:
-        put.wait()
+    keep.wait()
+
 
 def local(sizes, density, table_index, opacity_table, color_table, light_direction, shear_offsets):
     slices, rows, cols = density.shape
@@ -394,9 +369,9 @@
     f32, i32 = jnp.float32, jnp.int32
     dma = pltpu.SemaphoreType.DMA
     turned = jnp.transpose(shear_offsets, (0, 2, 1))
-    return pl.pallas_call(
+    layers = pl.pallas_call(
         functools.partial(kernel, sizes),
-        out_shape=jax.ShapeDtypeStruct((1, 4, rows, cols), f32),
+        out_shape=pltpu.VMEM((nd, 4, rows, cols), f32),
         in_specs=[pl.BlockSpec(memory_space=pl.ANY)] * 6,
         out_specs=pl.BlockSpec(memory_space=pl.ANY),
         scratch_shapes=[
@@ -412,13 +387,17 @@
             pltpu.VMEM((2, 3, 2, SUB, LANES), f32),
             pltpu.VMEM((7, slices, wide // LANES, rows + 2 * MAXS, LANES), f32),
             pltpu.VMEM((nd, 4, rows, cols), f32),
-            pltpu.VMEM((nd, 4, rows, cols), f32),
-            pltpu.VMEM((1, 4, rows, cols), f32),
             dma((len(DIRS),)), dma((len(DIRS),)), dma((len(DIRS),)), dma((len(DIRS),)),
             dma((nd, 4)), dma((nd, 4)),
         ],
-        compiler_params=pltpu.CompilerParams(collective_id=0, has_side_effects=True),
+        compiler_params=pltpu.CompilerParams(
+            collective_id=0, has_side_effects=True
+        ),
     )(density, table_index, opacity_table, color_table, light_direction, turned)
+    image = layers[0:1]
+    for k in range(1, nd):
+        image = image + (1.0 - image[:, 0:1]) * layers[k:k + 1]
+    return image
 
 
 def solution(mesh):

time: 21.5 us -> 20.1 us (0.935)
  local copies, waits for them, and re-layouts: 1.57 us -> 0 us
  other arithmetic: 0 us -> 0.76 us
  Pallas kernels: 19.8 us -> 19.2 us
    unnamed x1 -> x0, local copies, waits for them, and re-layouts: 1.57 us -> none
    add x0 -> x3, other arithmetic: none -> 0.74 us  [local(): image = image + (1.0 - image[:, 0:1]) * layers[k:k + 1]]
    pallas_call x1, Pallas kernels: 19.8 us -> 19.2 us  [local(): pl.pallas_call(functools.partial(kernel, sizes), out_shape=pltpu.VMEM((nd...]
where the time goes in v1:
time: 20.1 us; the launch traced here: 20 us
  Pallas kernels  19.2 us (96%)
  other arithmetic  0.76 us (4%)
    pallas_call x1, Pallas kernels, local(): pl.pallas_call(functools.partial(kernel, sizes), out_shape=pltpu.VMEM((nd...  19.2 us
    add x3, other arithmetic, local(): image = image + (1.0 - image[:, 0:1]) * layers[k:k + 1]  0.74 us

profile of v1, /device:TPU:0, one launch (start us, length us, event | category | flops | bytes accessed | tf_op | source)
XLA Modules:
  0.0 20.0 jit_solution(7704027681311764967)
XLA Ops:
  0.0 19.2 %shard_map.64 = f32[4,4,32,256]{3,2,1,0:T(8,128)S(1)} custom-call(f32[4,32,256]{2,1,0:T(8,128)} %dens_in.1, s32[4,32,256]{2,1,0:T(8,128)} %index_in.1, f32[256]{0:T(256)} %opacity_in.1, f32[3,256]{1,0:T(4,128)} %color_in.1, f32[4,3]{1,0:T(4,128)} %light_in.1, s32[4,2,16]{2,1,0:T(2,128)} %bitcast.7), custom_call_target="tpu_custom_call" | custom-call | tf_op jit(solution)/shard_map/pallas_call | solution.py:372
  19.3 0.7 %multiply_add_fusion = f32[1,4,32,256]{3,2,1,0:T(8,128)} fusion(f32[1,4,32,256]{3,2,1,0:T(8,128)S(1)} %multiply_add_fusion.1, f32[4,4,32,256]{3,2,1,0:T(8,128)S(1)} %shard_map.64, f32[32,256]{1,0:T(8,128)S(1)} %fusion), kind=kLoop, calls=%fused_computation | loop fusion | flops 65536 | bytes 425984 | tf_op jit(solution)/shard_map/add | solution.py:399
  (5 shorter events, 0.1 us)

commit v2 on v1

--- a/solution.py
+++ b/solution.py
@@ -54,9 +54,10 @@
         return tuple(pos + s for pos, s in zip(me, step))
 
     masks = list(range(nd - 1, 0, -1))
+    direct = [step for step in DIRS if step[0] == 0 or step[1] == 0 or step[2] != 0]
     barrier = pltpu.get_barrier_semaphore()
     count = jnp.int32(0)
-    for step in DIRS:
+    for step in direct:
         ok = there(step)
 
         @pl.when(ok)
@@ -112,7 +113,11 @@
 
     def copies(number, step, only_dst=False):
         z, x, y = step
+        relay = step not in direct
         side = 0 if y > 0 else 1
+        edge = slices - 1 if z > 0 else 0
+        slot = 0 if z > 0 else 1
+        put = 0 if z > 0 else slices + 1
         if z == 0 and y == 0:
             pairs = [
                 (wide_d.at[pl.ds(1, slices), src_rows(x, halo), pl.ds(0, cols)],
@@ -121,41 +126,58 @@
             ]
         elif z == 0:
             pairs = [
-                (edges[0].at[side], got_edges[0].at[x + 1, side]),
-                (edges[1].at[side], got_edges[1].at[x + 1, side]),
+                (got.at[1, side] if relay else own_edges.at[side], got.at[x + 1, side])
+                for own_edges, got in zip(edges, got_edges)
             ]
+        elif y == 0:
+            pairs = [(
+                wide_d.at[put if relay else edge + 1, src_rows(x, MAXS), pl.ds(0, cols)],
+                wide_d.at[put, dst_rows(x, MAXS), pl.ds(0, cols)],
+            )]
         else:
-            edge = slices - 1 if z > 0 else 0
-            slot = 0 if z > 0 else 1
-            if y == 0:
-                pairs = [(
-                    wide_d.at[edge + 1, src_rows(x, MAXS), pl.ds(0, cols)],
-                    wide_d.at[0 if z > 0 else slices + 1, dst_rows(x, MAXS), pl.ds(0, cols)],
-                )]
-            else:
-                pairs = [(edges[0].at[side, edge], got_depth.at[slot, x + 1, side])]
+            pairs = [(
+                got_depth.at[slot, 1, side] if relay else edges[0].at[side, edge], got_depth.at[slot, x + 1, side],
+            )]
         if only_dst:
             return [dst for _src, dst in pairs]
         made = []
         for (src, dst), (ss, rs) in zip(pairs, ((send_sem, recv_sem), (send2, recv2))):
             made.append(pltpu.make_async_remote_copy(
                 src_ref=src, dst_ref=dst, send_sem=ss.at[number], recv_sem=rs.at[number],
-                device_id=dev(step), device_id_type=pl.DeviceIdType.MESH,
+                device_id=dev((0, x, 0) if relay else step), device_id_type=pl.DeviceIdType.MESH,
             ))
         return made
 
+    def sends(step):
+        if step in direct:
+            return there(step)
+        z, x, y = step
+        return jnp.logical_and(there((0, x, 0)), there((-z, 0, -y)))
+
+    def launch(steps):
+        for step in steps:
+            @pl.when(sends(step))
+            def _():
+                for copy in copies(DIRS.index(step), step):
+                    copy.start()
+
+    def arrive(steps):
+        for step in steps:
+            @pl.when(there(tuple(-s for s in step)))
+            def _():
+                for copy in copies(DIRS.index(step), step):
+                    copy.wait_recv()
+
+    def relays(z, y):
+        return [(z, x, y) for x in (-1, 1)]
+
+    def relay(steps):
+        launch([step for step in steps if step not in direct])
+
     pl.semaphore_wait(barrier, count)
-    order = sorted(range(len(DIRS)), key=lambda k: -sum(abs(s) for s in DIRS[k]))
-    for number in order:
-        step = DIRS[number]
-
-        @pl.when(there(step))
-        def _():
-            for copy in copies(number, step):
-                copy.start()
-
-    for number in order:
-        step = DIRS[number]
+    launch(sorted(direct, key=lambda step: -sum(abs(s) for s in step)))
+
+    for number, step in enumerate(DIRS):
         back = tuple(-s for s in step)
 
         @pl.when(jnp.logical_not(there(back)))
@@ -216,9 +238,9 @@
     own = [
         (t, j) for t in range(MAXS // SUB, (MAXS + rows) // SUB) for j in range(tiles)
     ]
-    rest = [
-        (t, j) for t in range(wide_tiles) for j in range(tiles + 1) if (t, j) not in own
-    ]
+    beside = [(t, j) for t in range(wide_tiles) for j in range(tiles) if (t, j) not in own]
+    edge_own = [(t, tiles) for t in range(MAXS // SUB, (MAXS + rows) // SUB)]
+    edge_rest = [(t, tiles) for t in range(wide_tiles) if (t, tiles) not in edge_own]
 
     def over_slices(first, last, body):
         def step(z, carry):
@@ -234,19 +256,8 @@
 
         over_slices(0, slices, body)
 
-    def arrive(depth):
-        for number in reversed(order):
-            step = DIRS[number]
-            if (step[0] != 0) != depth:
-                continue
-
-            @pl.when(there(tuple(-s for s in step)))
-            def _():
-                for copy in copies(number, step):
-                    copy.wait_recv()
-
-    def unpack(depth):
-        for x in STEPS:
+    def unpack(depth, steps):
+        for x in steps:
             first, last = (rows - halo, rows) if x > 0 else ((0, halo) if x < 0 else (0, rows))
             base = 0 if x > 0 else (high if x < 0 else low)
             if depth:
@@ -271,12 +282,25 @@
                     target[at:at + SUB, cols:wide] = jnp.where(lane < LANES // 2, rr, ll)
 
     look_all(own)
-    arrive(False)
-    unpack(False)
-    look_all(rest)
+    arrive([(0, x, 0) for x in (-1, 1)])
+    look_all(beside)
+    arrive([(z, 0, 0) for z in (-1, 1)])
+    relay(relays(-1, 0) + relays(1, 0))
+    for y in (-1, 1):
+        arrive([(0, 0, y)])
+        relay(relays(0, y))
+    unpack(False, (0,))
+    look_all(edge_own)
+    for z in (-1, 1):
+        for y in (-1, 1):
+            arrive([(z, 0, y)])
+            relay(relays(z, y))
+    arrive(relays(0, -1) + relays(0, 1))
+    unpack(False, (-1, 1))
+    look_all(edge_rest)
     over_slices(1, slices - 1, slopes)
-    arrive(True)
-    unpack(True)
+    arrive([step for z in (-1, 1) for y in STEPS for step in relays(z, y)])
+    unpack(True, STEPS)
     slopes(0)
     if slices > 1:
         slopes(slices - 1)
@@ -344,10 +368,8 @@
     partial(0, 0, rows // SUB)
     keep = pltpu.make_async_copy(parts.at[0], others.at[d], in_sem.at[0])
     keep.start()
-    for number in order:
-        step = DIRS[number]
-
-        @pl.when(there(step))
+    for number, step in enumerate(DIRS):
+        @pl.when(sends(step))
         def _():
             for copy in copies(number, step):
                 copy.wait_send()

time: 20.1 us -> 20 us (level)
  no operation moved by 1% of the time
where the time goes in v2:
time: 20 us; the launch traced here: 19.8 us
  Pallas kernels  19 us (95%)
  other arithmetic  0.76 us (4%)
    pallas_call x1, Pallas kernels, local(): pl.pallas_call(functools.partial(kernel, sizes), out_shape=pltpu.VMEM((nd...  19 us
    add x3, other arithmetic, local(): image = image + (1.0 - image[:, 0:1]) * layers[k:k + 1]  0.74 us

profile of v2, /device:TPU:0, one launch (start us, length us, event | category | flops | bytes accessed | tf_op | source)
XLA Modules:
  0.0 19.8 jit_solution(15801615479552216956)
XLA Ops:
  0.0 19.0 %shard_map.64 = f32[4,4,32,256]{3,2,1,0:T(8,128)S(1)} custom-call(f32[4,32,256]{2,1,0:T(8,128)} %dens_in.1, s32[4,32,256]{2,1,0:T(8,128)} %index_in.1, f32[256]{0:T(256)} %opacity_in.1, f32[3,256]{1,0:T(4,128)} %color_in.1, f32[4,3]{1,0:T(4,128)} %light_in.1, s32[4,2,16]{2,1,0:T(2,128)} %bitcast.7), custom_call_target="tpu_custom_call" | custom-call | tf_op jit(solution)/shard_map/pallas_call | solution.py:394
  19.2 0.7 %multiply_add_fusion = f32[1,4,32,256]{3,2,1,0:T(8,128)} fusion(f32[1,4,32,256]{3,2,1,0:T(8,128)S(1)} %multiply_add_fusion.1, f32[4,4,32,256]{3,2,1,0:T(8,128)S(1)} %shard_map.64, f32[32,256]{1,0:T(8,128)S(1)} %fusion), kind=kLoop, calls=%fused_computation | loop fusion | flops 65536 | bytes 425984 | tf_op jit(solution)/shard_map/add | solution.py:421
  (5 shorter events, 0.1 us)

commit v3 on v2

--- a/solution.py
+++ b/solution.py
@@ -30,7 +30,7 @@
 
 def kernel(
     sizes, dens_in, index_in, opacity_in, color_in, light_in, shear_in, others,
-    opacity, color, light, shear, in_sem, wide_d, wide_i, edges, got_edges, got_depth, shaded, parts,
+    opacity, color, light, shear, in_sem, wide_d, wide_i, edges, ends, got_edges, got_depth, shaded, parts,
     send_sem, recv_sem, send2, recv2, part_send, part_recv,
 ):
     nd, nx, ny = sizes
@@ -95,15 +95,27 @@
     group = lane // GROUP
     for side in range(2):
         tile = tiles - 1 if side == 0 else 0
-        for number, (ref, buf) in enumerate(((wide_d, 0), (wide_i, 1))):
-            for z in range(slices):
+        for ref, buf in ((wide_d, 0), (wide_i, 1)):
+            last = [None, None]
+            for r in range(rows // SUB):
                 packed = None
-                for r in range(rows // SUB):
+                for z in range(slices):
                     v = ref[z + 1 - buf, low + r * SUB:low + (r + 1) * SUB, tile * LANES:(tile + 1) * LANES]
-                    shift = (GROUP * r + (GROUP if side == 0 else 0)) % LANES
-                    v = pltpu.roll(v, shift, 1) if shift else v
-                    packed = v if packed is None else jnp.where(group == r, v, packed)
-                edges[buf][side, z] = packed
+                    for place, into in ((z, None),) + ((((r, 0),) if z == 0 else ()) + (((r, 1),) if z == slices - 1 else ()) if buf == 0 else ()):
+                        shift = (GROUP * place + (GROUP if side == 0 else 0)) % LANES
+                        w = pltpu.roll(v, shift, 1) if shift else v
+                        if into is None:
+                            packed = w if packed is None else jnp.where(group == place, w, packed)
+                        else:
+                            last[into] = w if last[into] is None else jnp.where(group == place, w, last[into])
+                edges[buf][side, r] = packed
+            if buf == 0:
+                for into in range(2):
+                    ends[side, into] = last[into]
+
+    def tiles_of(x, reach):
+        n = reach // SUB
+        return pl.ds(rows // SUB - n, n) if x > 0 else (pl.ds(0, n) if x < 0 else pl.ds(0, rows // SUB))
 
     def src_rows(x, reach):
         return pl.ds(high - reach, reach) if x > 0 else (pl.ds(low, reach) if x < 0 else pl.ds(low, rows))
@@ -126,8 +138,8 @@
             ]
         elif z == 0:
             pairs = [
-                (got.at[1, side] if relay else own_edges.at[side], got.at[x + 1, side])
-                for own_edges, got in zip(edges, got_edges)
+                (own_edges.at[side, tiles_of(x, reach)], got.at[x + 1, side, tiles_of(x, reach)])
+                for own_edges, got, reach in zip(edges, got_edges, (halo, MAXS))
             ]
         elif y == 0:
             pairs = [(
@@ -136,7 +148,7 @@
             )]
         else:
             pairs = [(
-                got_depth.at[slot, 1, side] if relay else edges[0].at[side, edge], got_depth.at[slot, x + 1, side],
+                got_depth.at[slot, 1, side] if relay else ends.at[side, 1 if z > 0 else 0], got_depth.at[slot, x + 1, side],
             )]
         if only_dst:
             return [dst for _src, dst in pairs]
@@ -260,26 +272,28 @@
         for x in steps:
             first, last = (rows - halo, rows) if x > 0 else ((0, halo) if x < 0 else (0, rows))
             base = 0 if x > 0 else (high if x < 0 else low)
-            if depth:
-                jobs = [
-                    (got_depth.at[slot, x + 1], wide_d.at[slot * (slices + 1)]) for slot in range(2)
-                ]
-                jobs = [(got.at[0], got.at[1], target) for got, target in jobs]
-            else:
-                jobs = [
-                    (got.at[x + 1, 0, z], got.at[x + 1, 1, z], target.at[z + skip])
-                    for got, target, skip in ((got_edges[0], wide_d, 1), (got_edges[1], wide_i, 0))
-                    for z in range(slices)
-                ]
-            for from_left, from_right, target in jobs:
+            jobs = []
+            for r in range(first // SUB, last // SUB):
+                at = base + r * SUB - first
+                if depth:
+                    jobs += [
+                        (got_depth.at[slot, x + 1, 0], got_depth.at[slot, x + 1, 1], r, wide_d.at[slot * (slices + 1)], at)
+                        for slot in range(2)
+                    ]
+                    continue
+                for got, target, skip, reach in ((got_edges[0], wide_d, 1, halo), (got_edges[1], wide_i, 0, MAXS)):
+                    if (x > 0 and r < (rows - reach) // SUB) or (x < 0 and r >= reach // SUB):
+                        continue
+                    jobs += [
+                        (got.at[x + 1, 0, r], got.at[x + 1, 1, r], z, target.at[z + skip], at) for z in range(slices)
+                    ]
+            for from_left, from_right, place, target, at in jobs:
                 left, right = from_left[...], from_right[...]
-                for r in range(first // SUB, last // SUB):
-                    a = (LANES - GROUP * r) % LANES
-                    b = (LANES - GROUP - GROUP * r) % LANES
-                    rr = pltpu.roll(right, a, 1) if a else right
-                    ll = pltpu.roll(left, b, 1) if b else left
-                    at = base + r * SUB - first
-                    target[at:at + SUB, cols:wide] = jnp.where(lane < LANES // 2, rr, ll)
+                a = (LANES - GROUP * place) % LANES
+                b = (LANES - GROUP - GROUP * place) % LANES
+                rr = pltpu.roll(right, a, 1) if a else right
+                ll = pltpu.roll(left, b, 1) if b else left
+                target[at:at + SUB, cols:wide] = jnp.where(lane < LANES // 2, rr, ll)
 
     look_all(own)
     arrive([(0, x, 0) for x in (-1, 1)])
@@ -385,7 +399,7 @@
     slices, rows, cols = density.shape
     views = light_direction.shape[0]
     nd = sizes[0]
-    assert views == nd and rows // SUB * GROUP == LANES
+    assert views == nd and rows // SUB * GROUP == LANES and slices * GROUP <= LANES
     wide = cols + LANES
     halo = -(-(MAXS + 1) // SUB) * SUB
     f32, i32 = jnp.float32, jnp.int32
@@ -404,8 +418,9 @@
             dma((6,)),
             pltpu.VMEM((slices + 2, rows + 2 * halo, wide), f32),
             pltpu.VMEM((slices, rows + 2 * halo, wide), i32),
-            [pltpu.VMEM((2, slices, SUB, LANES), f32), pltpu.VMEM((2, slices, SUB, LANES), i32)],
-            [pltpu.VMEM((3, 2, slices, SUB, LANES), f32), pltpu.VMEM((3, 2, slices, SUB, LANES), i32)],
+            [pltpu.VMEM((2, rows // SUB, SUB, LANES), f32), pltpu.VMEM((2, rows // SUB, SUB, LANES), i32)],
+            pltpu.VMEM((2, 2, SUB, LANES), f32),
+            [pltpu.VMEM((3, 2, rows // SUB, SUB, LANES), f32), pltpu.VMEM((3, 2, rows // SUB, SUB, LANES), i32)],
             pltpu.VMEM((2, 3, 2, SUB, LANES), f32),
             pltpu.VMEM((7, slices, wide // LANES, rows + 2 * MAXS, LANES), f32),
             pltpu.VMEM((nd, 4, rows, cols), f32),

time: 20 us -> 19.8 us (0.990)
    pallas_call x1, Pallas kernels: 19 us -> 18.8 us  [local(): pl.pallas_call(functools.partial(kernel, sizes), out_shape=pltpu.VMEM((nd...]
where the time goes in v3:
time: 19.8 us; the launch traced here: 19.6 us
  Pallas kernels  18.8 us (95%)
  other arithmetic  0.76 us (4%)
    pallas_call x1, Pallas kernels, local(): pl.pallas_call(functools.partial(kernel, sizes), out_shape=pltpu.VMEM((nd...  18.8 us
    add x3, other arithmetic, local(): image = image + (1.0 - image[:, 0:1]) * layers[k:k + 1]  0.74 us

profile of v3, /device:TPU:0, one launch (start us, length us, event | category | flops | bytes accessed | tf_op | source)
XLA Modules:
  0.0 19.6 jit_solution(14462270135630225617)
XLA Ops:
  0.0 18.8 %shard_map.64 = f32[4,4,32,256]{3,2,1,0:T(8,128)S(1)} custom-call(f32[4,32,256]{2,1,0:T(8,128)} %dens_in.1, s32[4,32,256]{2,1,0:T(8,128)} %index_in.1, f32[256]{0:T(256)} %opacity_in.1, f32[3,256]{1,0:T(4,128)} %color_in.1, f32[4,3]{1,0:T(4,128)} %light_in.1, s32[4,2,16]{2,1,0:T(2,128)} %bitcast.7), custom_call_target="tpu_custom_call" | custom-call | tf_op jit(solution)/shard_map/pallas_call | solution.py:408
  18.9 0.7 %multiply_add_fusion = f32[1,4,32,256]{3,2,1,0:T(8,128)} fusion(f32[1,4,32,256]{3,2,1,0:T(8,128)S(1)} %multiply_add_fusion.1, f32[4,4,32,256]{3,2,1,0:T(8,128)S(1)} %shard_map.64, f32[32,256]{1,0:T(8,128)S(1)} %fusion), kind=kLoop, calls=%fused_computation | loop fusion | flops 65536 | bytes 425984 | tf_op jit(solution)/shard_map/add | solution.py:436
  (5 shorter events, 0.1 us)
